TPU v7x, 32 devices: a whole 2x2x4 slice. The times are simulated.
32 devices in a mesh: shard: 2 (over y), ctx: 4 (over x, core), tp: 4 (over z).
Axes of the slice: x: 2, y: 2, z: 4, core: 2. Of those that a mesh axis runs over, the one named last changes fastest.
Arguments:
- video: bfloat16 [2, 16, 16, 16, 1152], P('shard', 'ctx', 'tp'), may hold values from -6 to 6
- cond: bfloat16 [2, 1152], P('shard'), may hold values from -6 to 6
- w_ada: bfloat16 [2, 1152, 6912], P(None, 'shard', 'tp'), may hold values from -0.1875 to 0.1875
- b_ada: bfloat16 [2, 6912], P(None, 'tp'), may hold values from 0.5 to 1.5
- w_qkv: bfloat16 [2, 3, 1152, 1152], P(None, None, 'shard', 'tp'), may hold values from -0.09375 to 0.09375
- b_qv: bfloat16 [2, 2, 1152], P(None, None, 'tp'), may hold values from -3 to 3
- w_out: bfloat16 [2, 1152, 1152], P(None, 'tp', 'shard'), may hold values from -0.75 to 0.75
- b_out: bfloat16 [2, 1152], replicated, may hold values from -3 to 3
- w_up: bfloat16 [2, 1152, 4608], P(None, 'shard', 'tp'), may hold values from -0.09375 to 0.09375
- b_up: bfloat16 [2, 4608], P(None, 'tp'), may hold values from -3 to 3
- w_down: bfloat16 [2, 4608, 1152], P(None, 'tp', 'shard'), may hold values from -0.09375 to 0.09375
- b_down: bfloat16 [2, 1152], replicated, may hold values from -3 to 3
- cotangent: bfloat16 [2, 16, 16, 16, 1152], P('shard', None, 'tp', 'ctx'), may hold values from -6 to 6
Outputs:
- out: bfloat16 [2, 16, 16, 16, 1152], P('shard', None, 'tp', 'ctx')
- grad_video: float32 [2, 16, 16, 16, 1152], P('shard', 'ctx', 'tp')
- grad_cond: float32 [2, 1152], P('shard')
- grad_w_ada: float32 [2, 1152, 6912], P(None, 'shard', 'tp')
- grad_b_ada: float32 [2, 6912], P(None, 'tp')
- grad_w_qkv: float32 [2, 3, 1152, 1152], P(None, None, 'shard', 'tp')
- grad_b_qv: float32 [2, 2, 1152], P(None, None, 'tp')
- grad_w_out: float32 [2, 1152, 1152], P(None, 'tp', 'shard')
- grad_b_out: float32 [2, 1152], replicated
- grad_w_up: float32 [2, 1152, 4608], P(None, 'shard', 'tp')
- grad_b_up: float32 [2, 4608], P(None, 'tp')
- grad_w_down: float32 [2, 4608, 1152], P(None, 'tp', 'shard')
- grad_b_down: float32 [2, 1152], replicated
All inputs are finite; a program needn't handle non-finite values.
Results may differ from a plain program's by a relative error of at most 0.025.
Values may be sent and summed in bfloat16 or wider, within the bound.
No kernel may reach another device: no remote copies, remote signals or barrier semaphores. Data moves between devices by JAX's collectives and lax.ppermute only.
A program may use at most 256 MiB of HBM per device.

v0:
```python
from functools import partial
import math
import jax
import jax.numpy as jnp
from jax import lax
from jax.sharding import PartitionSpec as P

HEAD_DIM = 72
highest = lax.Precision.HIGHEST


def layer_norm(values):
    average = jnp.mean(values, axis=-1, keepdims=True)
    centered = values - average
    spread = jnp.mean(centered * centered, axis=-1, keepdims=True)
    return centered * lax.rsqrt(spread + 1e-06)


def modulate(values, offset, factor):
    return layer_norm(values) * (1.0 + factor) + offset


def split_mod(modulation):
    pieces = modulation.reshape(modulation.shape[0], 6, 1, 1, 1, modulation.shape[1] // 6)
    return [pieces[:, number] for number in range(6)]


def to_sequences(rows, grid, temporal):
    heads = rows.reshape(grid + (-1, HEAD_DIM))
    head_count = heads.shape[5]
    if temporal:
        heads = jnp.transpose(heads, (0, 1, 3, 4, 2, 5, 6))
        return heads.reshape(-1, grid[2], head_count, HEAD_DIM)
    heads = jnp.transpose(heads, (1, 2, 0, 3, 4, 5, 6))
    return heads.reshape(grid[1] * grid[2], -1, head_count, HEAD_DIM)


def from_sequences(heads, grid, temporal):
    head_count = heads.shape[2]
    if temporal:
        heads = heads.reshape(grid[0], grid[1], grid[3], grid[4], grid[2], head_count, HEAD_DIM)
        heads = jnp.transpose(heads, (0, 1, 4, 2, 3, 5, 6))
    else:
        heads = heads.reshape(grid[1], grid[2], grid[0], grid[3], grid[4], head_count, HEAD_DIM)
        heads = jnp.transpose(heads, (2, 0, 1, 3, 4, 5, 6))
    return heads.reshape(-1, head_count * HEAD_DIM)


def attend(query_seq, key_seq, value_seq):
    factor = 1.0 / math.sqrt(HEAD_DIM)
    scores = (
        jnp.einsum("bqhe,bkhe->bhqk", query_seq, key_seq, preferred_element_type=jnp.float32)
        * factor
    )
    row_max = jnp.max(scores, axis=-1, keepdims=True)
    weights = jnp.exp(scores - row_max)
    totals = jnp.sum(weights, axis=-1, keepdims=True)
    probs_low = (weights / totals).astype(jnp.bfloat16)
    attended = jnp.einsum(
        "bhqk,bkhe->bqhe", probs_low, value_seq, preferred_element_type=jnp.float32
    )
    return (attended.astype(jnp.bfloat16), row_max + jnp.log(totals))


def attend_back(query_seq, key_seq, value_seq, log_total, grad_out):
    factor = 1.0 / math.sqrt(HEAD_DIM)
    scores = (
        jnp.einsum("bqhe,bkhe->bhqk", query_seq, key_seq, preferred_element_type=jnp.float32)
        * factor
    )
    probs = jnp.exp(scores - log_total)
    grad_value = jnp.einsum(
        "bhqk,bqhe->bkhe", probs.astype(jnp.bfloat16), grad_out, preferred_element_type=jnp.float32
    ).astype(jnp.bfloat16)
    grad_probs = jnp.einsum(
        "bqhe,bkhe->bhqk", grad_out, value_seq, preferred_element_type=jnp.float32
    )
    inner = jnp.sum(grad_probs * probs, axis=-1, keepdims=True)
    grad_scores = (probs * (grad_probs - inner)).astype(jnp.bfloat16)
    grad_query = (
        jnp.einsum("bhqk,bkhe->bqhe", grad_scores, key_seq, preferred_element_type=jnp.float32)
        * factor
    ).astype(jnp.bfloat16)
    grad_key = (
        jnp.einsum("bhqk,bqhe->bkhe", grad_scores, query_seq, preferred_element_type=jnp.float32)
        * factor
    ).astype(jnp.bfloat16)
    return (grad_query, grad_key, grad_value)


def fetch_forward(number, w_ada, w_qkv, w_out, w_up, w_down):
    return (
        lax.all_gather(w_ada[number], "shard", axis=0, tiled=True),
        lax.all_gather(w_qkv[number], "shard", axis=1, tiled=True),
        lax.all_gather(w_out[number], "shard", axis=1, tiled=True),
        lax.all_gather(w_up[number], "shard", axis=0, tiled=True),
        lax.all_gather(w_down[number], "shard", axis=1, tiled=True),
    )


def fetch_again(number, w_ada, w_qkv, w_out, w_up, w_down):
    return (
        lax.all_gather(w_ada[number], "shard", axis=0, tiled=True),
        lax.all_gather(w_qkv[number], "shard", axis=1, tiled=True),
        lax.all_gather(w_out[number], "shard", axis=1, tiled=True),
        lax.all_gather(w_up[number], "shard", axis=0, tiled=True),
        lax.all_gather(w_down[number], "shard", axis=1, tiled=True),
    )


def spread_rows(values):
    return lax.all_gather(values[None], "tp", axis=0, tiled=True)


def spread_grads(values):
    return lax.all_gather(values[None], "tp", axis=0, tiled=True)


def reduce_rows(term, own_rows):
    return lax.psum_scatter(
        term(jnp.int32(0), own_rows * lax.axis_size("tp")), "tp", scatter_dimension=0, tiled=True
    )


def reduce_grads(term, own_rows):
    return lax.psum_scatter(
        term(jnp.int32(0), own_rows * lax.axis_size("tp")), "tp", scatter_dimension=0, tiled=True
    )


def sum_weight_grads(grads):
    summed = (
        lax.psum_scatter(
            grads[0].astype(jnp.bfloat16), "shard", scatter_dimension=0, tiled=True
        ).astype(jnp.float32),
        lax.psum_scatter(
            grads[1].astype(jnp.bfloat16), "shard", scatter_dimension=1, tiled=True
        ).astype(jnp.float32),
        lax.psum_scatter(
            grads[2].astype(jnp.bfloat16), "shard", scatter_dimension=1, tiled=True
        ).astype(jnp.float32),
        lax.psum_scatter(
            grads[3].astype(jnp.bfloat16), "shard", scatter_dimension=0, tiled=True
        ).astype(jnp.float32),
        lax.psum_scatter(
            grads[4].astype(jnp.bfloat16), "shard", scatter_dimension=1, tiled=True
        ).astype(jnp.float32),
    )
    return (
        lax.psum(summed[0].astype(jnp.bfloat16), "ctx").astype(jnp.float32),
        lax.psum(summed[1].astype(jnp.bfloat16), "ctx").astype(jnp.float32),
        lax.psum(summed[2].astype(jnp.bfloat16), "ctx").astype(jnp.float32),
        lax.psum(summed[3].astype(jnp.bfloat16), "ctx").astype(jnp.float32),
        lax.psum(summed[4].astype(jnp.bfloat16), "ctx").astype(jnp.float32),
    )


def row_product(left, right, first_row, row_count):
    return jnp.dot(left, right, preferred_element_type=jnp.float32)


def row_product_back(left, right, first_row, row_count):
    return jnp.einsum("rf,df->rd", left, right, preferred_element_type=jnp.float32)


def qkv_product_back(left, right, first_row, row_count):
    return jnp.einsum("trc,tdc->rd", left, right, preferred_element_type=jnp.float32)


def forward_block(inputs, cond_act, gathered, b_ada, b_qv, b_out, b_up, b_down, temporal):
    ada_full, qkv_full, out_full, up_full, down_full = gathered
    width = inputs.shape[-1]
    own_rows = inputs.shape[0] * inputs.shape[1] * inputs.shape[2] * inputs.shape[3]
    mod_part = jnp.dot(cond_act, ada_full, preferred_element_type=jnp.float32) + b_ada
    modulation = lax.all_gather(mod_part, "tp", axis=1, tiled=True)
    shift_a, scale_a, gate_a, shift_m, scale_m, gate_m = split_mod(modulation)
    hidden = spread_rows(modulate(inputs, shift_a, scale_a).astype(jnp.bfloat16))
    grid = hidden.shape[:5]
    hidden_rows = hidden.reshape(-1, width)
    projected = jnp.einsum("rd,tdc->trc", hidden_rows, qkv_full, preferred_element_type=jnp.float32)
    query_seq = to_sequences((projected[0] + b_qv[0]).astype(jnp.bfloat16), grid, temporal)
    key_seq = to_sequences(projected[1].astype(jnp.bfloat16), grid, temporal)
    value_seq = to_sequences((projected[2] + b_qv[1]).astype(jnp.bfloat16), grid, temporal)
    attended, log_total = attend(query_seq, key_seq, value_seq)
    attended_rows = from_sequences(attended, grid, temporal)
    attn_out = (
        reduce_rows(partial(row_product, attended_rows, out_full), own_rows) + b_out
    ).reshape(inputs.shape)
    after_attn = inputs + gate_a * attn_out
    hidden_two = spread_rows(modulate(after_attn, shift_m, scale_m).astype(jnp.bfloat16)).reshape(
        -1, width
    )
    up_rows = jnp.dot(hidden_two, up_full, preferred_element_type=jnp.float32) + b_up
    activated = jax.nn.gelu(up_rows, approximate=True).astype(jnp.bfloat16)
    mlp_out = (reduce_rows(partial(row_product, activated, down_full), own_rows) + b_down).reshape(
        inputs.shape
    )
    result = after_attn + gate_m * mlp_out
    kept = (
        inputs,
        after_attn,
        modulation,
        hidden_rows,
        query_seq,
        key_seq,
        value_seq,
        log_total,
        attended_rows,
        attn_out,
        hidden_two,
        up_rows,
        mlp_out,
        grid,
    )
    return (result, kept)


def backward_block(grad_y, kept, gathered, cond_act, temporal):
    (
        inputs,
        after_attn,
        modulation,
        hidden_rows,
        query_seq,
        key_seq,
        value_seq,
        log_total,
        attended_rows,
        attn_out,
        hidden_two,
        up_rows,
        mlp_out,
        grid,
    ) = kept
    ada_full, qkv_full, out_full, up_full, down_full = gathered
    width = inputs.shape[-1]
    clips = inputs.shape[0]
    own_rows = inputs.shape[0] * inputs.shape[1] * inputs.shape[2] * inputs.shape[3]
    shift_a, scale_a, gate_a, shift_m, scale_m, gate_m = split_mod(modulation)
    token_axes = (1, 2, 3)
    grad_mlp = (gate_m * grad_y).astype(jnp.bfloat16)
    grad_gate_m = jnp.sum(grad_y * mlp_out, axis=token_axes)
    grad_mlp_rows = spread_grads(grad_mlp).reshape(-1, width)
    grad_b_down = jnp.sum(grad_mlp_rows, axis=0, dtype=jnp.float32)
    activated, gelu_back = jax.vjp(partial(jax.nn.gelu, approximate=True), up_rows)
    grad_w_down = jnp.einsum(
        "rf,rd->fd",
        activated.astype(jnp.bfloat16),
        grad_mlp_rows,
        preferred_element_type=jnp.float32,
    )
    grad_act = jnp.einsum("rd,fd->rf", grad_mlp_rows, down_full, preferred_element_type=jnp.float32)
    grad_up = gelu_back(grad_act)[0].astype(jnp.bfloat16)
    grad_b_up = jnp.sum(grad_up, axis=0, dtype=jnp.float32)
    grad_w_up = jnp.einsum("rd,rf->df", hidden_two, grad_up, preferred_element_type=jnp.float32)
    grad_hidden_two = reduce_grads(partial(row_product_back, grad_up, up_full), own_rows).reshape(
        inputs.shape
    )
    unused_two, norm_back_two = jax.vjp(modulate, after_attn, shift_m, scale_m)
    grad_norm_two, grad_shift_m, grad_scale_m = norm_back_two(grad_hidden_two)
    grad_after = grad_y + grad_norm_two
    grad_attn = (gate_a * grad_after).astype(jnp.bfloat16)
    grad_gate_a = jnp.sum(grad_after * attn_out, axis=token_axes)
    grad_attn_rows = spread_grads(grad_attn).reshape(-1, width)
    grad_b_out = jnp.sum(grad_attn_rows, axis=0, dtype=jnp.float32)
    grad_w_out = jnp.einsum(
        "rc,rd->cd", attended_rows, grad_attn_rows, preferred_element_type=jnp.float32
    )
    grad_attended = jnp.einsum(
        "rd,cd->rc", grad_attn_rows, out_full, preferred_element_type=jnp.float32
    ).astype(jnp.bfloat16)
    grad_query, grad_key, grad_value = attend_back(
        query_seq, key_seq, value_seq, log_total, to_sequences(grad_attended, grid, temporal)
    )
    grad_proj = jnp.stack(
        [
            from_sequences(grad_query, grid, temporal),
            from_sequences(grad_key, grid, temporal),
            from_sequences(grad_value, grid, temporal),
        ]
    )
    grad_b_qv = jnp.stack(
        [
            jnp.sum(grad_proj[0], axis=0, dtype=jnp.float32),
            jnp.sum(grad_proj[2], axis=0, dtype=jnp.float32),
        ]
    )
    grad_w_qkv = jnp.einsum(
        "rd,trc->tdc", hidden_rows, grad_proj, preferred_element_type=jnp.float32
    )
    grad_hidden = reduce_grads(partial(qkv_product_back, grad_proj, qkv_full), own_rows).reshape(
        inputs.shape
    )
    unused_one, norm_back_one = jax.vjp(modulate, inputs, shift_a, scale_a)
    grad_norm_one, grad_shift_a, grad_scale_a = norm_back_one(grad_hidden)
    grad_inputs = grad_after + grad_norm_one
    grad_mod = jnp.concatenate(
        [
            grad_shift_a.reshape(clips, width),
            grad_scale_a.reshape(clips, width),
            grad_gate_a,
            grad_shift_m.reshape(clips, width),
            grad_scale_m.reshape(clips, width),
            grad_gate_m,
        ],
        axis=1,
    )
    grad_mod_part = lax.psum_scatter(grad_mod, "tp", scatter_dimension=1, tiled=True)
    grad_w_ada = jnp.dot(cond_act.astype(jnp.float32).T, grad_mod_part, precision=highest)
    grad_b_ada = jnp.sum(grad_mod_part, axis=0)
    grad_cond_part = jnp.dot(grad_mod_part, ada_full.astype(jnp.float32).T, precision=highest)
    summed = sum_weight_grads((grad_w_ada, grad_w_qkv, grad_w_out, grad_w_up, grad_w_down))
    biases = (grad_b_ada, grad_b_qv, grad_b_out, grad_b_up, grad_b_down)
    return (grad_inputs, summed, biases, grad_cond_part)


def body(
    video, cond, w_ada, b_ada, w_qkv, b_qv, w_out, b_out, w_up, b_up, w_down, b_down, cotangent
):
    cond_float = cond.astype(jnp.float32)
    silu_value, silu_back = jax.vjp(jax.nn.silu, cond_float)
    cond_act = silu_value.astype(jnp.bfloat16)
    first = fetch_forward(0, w_ada, w_qkv, w_out, w_up, w_down)
    middle, kept_one = forward_block(
        video.astype(jnp.float32),
        cond_act,
        first,
        b_ada[0],
        b_qv[0],
        b_out[0],
        b_up[0],
        b_down[0],
        False,
    )
    moved = lax.all_to_all(
        middle.astype(jnp.bfloat16), "ctx", split_axis=3, concat_axis=1, tiled=True
    )
    second = fetch_forward(1, w_ada, w_qkv, w_out, w_up, w_down)
    result, kept_two = forward_block(
        moved.astype(jnp.float32),
        cond_act,
        second,
        b_ada[1],
        b_qv[1],
        b_out[1],
        b_up[1],
        b_down[1],
        True,
    )
    second_back = fetch_again(1, w_ada, w_qkv, w_out, w_up, w_down)
    grad_moved, grads_two, biases_two, cond_two = backward_block(
        cotangent.astype(jnp.float32), kept_two, second_back, cond_act, True
    )
    grad_middle = lax.all_to_all(
        grad_moved.astype(jnp.bfloat16), "ctx", split_axis=1, concat_axis=3, tiled=True
    ).astype(jnp.float32)
    first_back = fetch_again(0, w_ada, w_qkv, w_out, w_up, w_down)
    grad_video, grads_one, biases_one, cond_one = backward_block(
        grad_middle, kept_one, first_back, cond_act, False
    )
    bias_sums = lax.psum(
        (
            jnp.stack([biases_one[0], biases_two[0]]),
            jnp.stack([biases_one[1], biases_two[1]]),
            jnp.stack([biases_one[2], biases_two[2]]),
            jnp.stack([biases_one[3], biases_two[3]]),
            jnp.stack([biases_one[4], biases_two[4]]),
        ),
        ("shard", "ctx"),
    )
    grad_act_total = lax.psum(cond_one + cond_two, ("ctx", "tp"))
    grad_cond = silu_back(grad_act_total)[0]
    return (
        result.astype(jnp.bfloat16),
        grad_video,
        grad_cond,
        jnp.stack([grads_one[0], grads_two[0]]),
        bias_sums[0],
        jnp.stack([grads_one[1], grads_two[1]]),
        bias_sums[1],
        jnp.stack([grads_one[2], grads_two[2]]),
        bias_sums[2],
        jnp.stack([grads_one[3], grads_two[3]]),
        bias_sums[3],
        jnp.stack([grads_one[4], grads_two[4]]),
        bias_sums[4],
    )


def solution(mesh):
    in_specs = (
        P("shard", "ctx", "tp", None, None),
        P("shard", None),
        P(None, "shard", "tp"),
        P(None, "tp"),
        P(None, None, "shard", "tp"),
        P(None, None, "tp"),
        P(None, "tp", "shard"),
        P(),
        P(None, "shard", "tp"),
        P(None, "tp"),
        P(None, "tp", "shard"),
        P(),
        P("shard", None, "tp", "ctx", None),
    )
    out_specs = (
        P("shard", None, "tp", "ctx", None),
        P("shard", "ctx", "tp", None, None),
        P("shard", None),
        P(None, "shard", "tp"),
        P(None, "tp"),
        P(None, None, "shard", "tp"),
        P(None, None, "tp"),
        P(None, "tp", "shard"),
        P(),
        P(None, "shard", "tp"),
        P(None, "tp"),
        P(None, "tp", "shard"),
        P(),
    )
    return jax.shard_map(body, mesh=mesh, in_specs=in_specs, out_specs=out_specs, check_vma=False)
```

profile of v0, /device:TPU:0, one launch (start us, length us, event | category | flops | bytes accessed | tf_op | source)
XLA Modules:
  0.0 2567.8 jit_solution(18138175500458335088)
XLA Ops:
  20.1 50.5 %all-gather.40.cloned.1.call-done = bf16[1,1152,1728]{2,1,0:T(8,128)(2,1)} async-done(((bf16[1,576,1728]{2,1,0:T(8,128)(2,1)}), bf16[1,1152,1728]{2,1,0:T(8,128)(2,1)}) %all-gather.40.cloned.1.call-update) | async-done | bytes 3981328 | tf_op jit(solution)/shard_map/all_gather | solution.py:93
  73.6 55.1 %all-gather.52.cloned.1.call-done = bf16[1,1152,1728]{2,1,0:T(8,128)(2,1)} async-done(((bf16[1,576,1728]{2,1,0:T(8,128)(2,1)}), bf16[1,1152,1728]{2,1,0:T(8,128)(2,1)}) %all-gather.52.cloned.1.call-update) | async-done | bytes 3981328 | tf_op jit(solution)/shard_map/all_gather | solution.py:93
  131.7 20.4 all-reduce.3
  156.8 40.7 %all-gather.4 = bf16[1,288,1152]{1,0,2:T(2,128)(2,1)S(1)} all-gather(bf16[1,288,576]{1,0,2:T(2,128)(2,1)S(1)} %copy.342), channel_id=6, replica_groups=mesh['shard'=2,'ctx'=4,'tp'=4] {'shard'}, dimensions={2}, use_global_device_ids=true | all-gather | bytes 995328 | tf_op jit(solution)/shard_map/all_gather | solution.py:95
  208.3 42.8 %all-gather.42.cloned.1.call-done = bf16[4,4,4,16,1152]{4,3,2,1,0:T(8,128)(2,1)} async-done(((bf16[1,4,4,16,1152]{4,3,2,1,0:T(8,128)(2,1)}), bf16[4,4,4,16,1152]{4,3,2,1,0:T(8,128)(2,1)}) %all-gather.42.cloned.1.call-update) | async-done | bytes 2359312 | tf_op jit(solution)/shard_map/all_gather | solution.py:112
  289.5 80.0 %reduce-scatter.33.cloned.1.call-done = f32[256,1152]{1,0:T(8,128)} async-done(((f32[1024,1152]{1,0:T(8,128)}), f32[256,1152]{1,0:T(8,128)}) %reduce-scatter.33.cloned.1.call-update) | async-done | bytes 1179664 | tf_op jit(solution)/shard_map/reduce_scatter | solution.py:120
  377.5 34.0 %all-gather.48.cloned.1.call-done = bf16[1,1152,1152]{2,1,0:T(8,128)(2,1)} async-done(((bf16[1,576,1152]{2,1,0:T(8,128)(2,1)}), bf16[1,1152,1152]{2,1,0:T(8,128)(2,1)}) %all-gather.48.cloned.1.call-update) | async-done | bytes 2654224 | tf_op jit(solution)/shard_map/all_gather | solution.py:96
  411.5 52.2 %all-gather.46.cloned.1.call-done = bf16[4,4,4,16,1152]{4,3,2,1,0:T(8,128)(2,1)} async-done(((bf16[1,4,4,16,1152]{4,3,2,1,0:T(8,128)(2,1)}), bf16[4,4,4,16,1152]{4,3,2,1,0:T(8,128)(2,1)}) %all-gather.46.cloned.1.call-update) | async-done | bytes 2359312 | tf_op jit(solution)/shard_map/all_gather | solution.py:112
  463.6 8.1 convolution_add_fusion.1
  471.8 32.1 %all-gather.50.cloned.1.call-done = bf16[1,1152,1152]{1,2,0:T(8,128)(2,1)} async-done(((bf16[1,1152,576]{1,2,0:T(8,128)(2,1)}), bf16[1,1152,1152]{1,2,0:T(8,128)(2,1)}) %all-gather.50.cloned.1.call-update) | async-done | bytes 2654224 | tf_op jit(solution)/shard_map/all_gather | solution.py:97
  503.9 9.6 fusion.37
  518.3 80.6 %reduce-scatter.35.cloned.1.call-done = f32[256,1152]{1,0:T(8,128)} async-done(((f32[1024,1152]{1,0:T(8,128)}), f32[256,1152]{1,0:T(8,128)}) %reduce-scatter.35.cloned.1.call-update) | async-done | bytes 1179664 | tf_op jit(solution)/shard_map/reduce_scatter | solution.py:120
  606.1 8.3 all-to-all-done
  628.0 41.5 %all-gather.11 = bf16[1,288,1152]{1,0,2:T(2,128)(2,1)S(1)} all-gather(bf16[1,288,576]{1,0,2:T(2,128)(2,1)} %copy.344), channel_id=13, replica_groups=mesh['shard'=2,'ctx'=4,'tp'=4] {'shard'}, dimensions={2}, use_global_device_ids=true | all-gather | bytes 995328 | tf_op jit(solution)/shard_map/all_gather | solution.py:95
  680.3 41.6 %all-gather.34.cloned.1.call-done = bf16[4,1,16,4,4,1152]{5,2,4,3,1,0:T(8,128)(2,1)} async-done(((bf16[1,1,16,4,4,1152]{5,2,4,3,1,0:T(8,128)(2,1)}), bf16[4,1,16,4,4,1152]{5,2,4,3,1,0:T(8,128)(2,1)}) %all-gather.34.cloned.1.call-update) | async-done | bytes 2359312 | tf_op jit(solution)/shard_map/all_gather | solution.py:112
  763.2 84.2 %reduce-scatter.37.cloned.1.call-done = f32[256,1152]{1,0:T(8,128)} async-done(((f32[1024,1152]{1,0:T(8,128)}), f32[256,1152]{1,0:T(8,128)}) %reduce-scatter.37.cloned.1.call-update) | async-done | bytes 1179664 | tf_op jit(solution)/shard_map/reduce_scatter | solution.py:120
  866.7 47.4 %all-gather.36.cloned.1.call-done = bf16[4,1,16,4,4,1152]{5,2,4,3,1,0:T(8,128)(2,1)} async-done(((bf16[1,1,16,4,4,1152]{5,2,4,3,1,0:T(8,128)(2,1)}), bf16[4,1,16,4,4,1152]{5,2,4,3,1,0:T(8,128)(2,1)}) %all-gather.36.cloned.1.call-update) | async-done | bytes 2359312 | tf_op jit(solution)/shard_map/all_gather | solution.py:112
  923.6 30.1 %all-gather.56.cloned.1.call-done = bf16[1,1152,1152]{2,1,0:T(8,128)(2,1)} async-done(((bf16[1,576,1152]{2,1,0:T(8,128)(2,1)}), bf16[1,1152,1152]{2,1,0:T(8,128)(2,1)}) %all-gather.56.cloned.1.call-update) | async-done | bytes 2654224 | tf_op jit(solution)/shard_map/all_gather | solution.py:96
  953.7 8.1 convolution_add_fusion
  961.8 32.6 %all-gather.58.cloned.1.call-done = bf16[1,1152,1152]{1,2,0:T(8,128)(2,1)} async-done(((bf16[1,1152,576]{1,2,0:T(8,128)(2,1)}), bf16[1,1152,1152]{1,2,0:T(8,128)(2,1)}) %all-gather.58.cloned.1.call-update) | async-done | bytes 2654224 | tf_op jit(solution)/shard_map/all_gather | solution.py:97
  994.5 9.5 fusion.28
  1004.0 42.4 %all-gather.60.cloned.1.call-done = bf16[4,16,4,4,1152]{4,1,3,2,0:T(8,128)(2,1)} async-done(((bf16[1,16,4,4,1152]{4,1,3,2,0:T(8,128)(2,1)}), bf16[4,16,4,4,1152]{4,1,3,2,0:T(8,128)(2,1)}) %all-gather.60.cloned.1.call-update) | async-done | bytes 2359312 | tf_op jit(solution)/shard_map/all_gather | solution.py:116
  1055.4 9.1 convert_reduce_fusion.4
  1079.1 53.6 %reduce-scatter.39.cloned.1.call-done = f32[256,1152]{1,0:T(8,128)} async-done(((f32[1024,1152]{1,0:T(8,128)}), f32[256,1152]{1,0:T(8,128)}) %reduce-scatter.39.cloned.1.call-update) | async-done | bytes 1179664 | tf_op jit(solution)/shard_map/reduce_scatter | solution.py:120
  1137.6 83.6 %reduce-scatter.41.cloned.1.call-done = f32[256,1152]{1,0:T(8,128)} async-done(((f32[1024,1152]{1,0:T(8,128)}), f32[256,1152]{1,0:T(8,128)}) %reduce-scatter.41.cloned.1.call-update) | async-done | bytes 1179664 | tf_op jit(solution)/shard_map/reduce_scatter | solution.py:126
  1241.0 49.7 %all-gather.62.cloned.1.call-done = bf16[4,16,4,4,1152]{4,1,3,2,0:T(8,128)(2,1)} async-done(((bf16[1,16,4,4,1152]{4,1,3,2,0:T(8,128)(2,1)}), bf16[4,16,4,4,1152]{4,1,3,2,0:T(8,128)(2,1)}) %all-gather.62.cloned.1.call-update) | async-done | bytes 2359312 | tf_op jit(solution)/shard_map/all_gather | solution.py:116
  1338.0 82.7 %reduce-scatter.43.cloned.1.call-done = f32[256,1152]{1,0:T(8,128)} async-done(((f32[1024,1152]{1,0:T(8,128)}), f32[256,1152]{1,0:T(8,128)}) %reduce-scatter.43.cloned.1.call-update) | async-done | bytes 1179664 | tf_op jit(solution)/shard_map/reduce_scatter | solution.py:126
  1439.7 12.1 all_to_all.8
  1453.4 49.7 %all-gather.38.cloned.1.call-done = bf16[4,1,4,4,16,1152]{5,4,3,2,1,0:T(8,128)(2,1)} async-done(((bf16[1,1,4,4,16,1152]{5,4,3,2,1,0:T(8,128)(2,1)}), bf16[4,1,4,4,16,1152]{5,4,3,2,1,0:T(8,128)(2,1)}) %all-gather.38.cloned.1.call-update) | async-done | bytes 2359312 | tf_op jit(solution)/shard_map/all_gather | solution.py:116
  1503.1 9.6 convert_reduce_fusion.5
  1520.9 82.7 %reduce-scatter.45.cloned.1.call-done = f32[256,1152]{1,0:T(8,128)} async-done(((f32[1024,1152]{1,0:T(8,128)}), f32[256,1152]{1,0:T(8,128)}) %reduce-scatter.45.cloned.1.call-update) | async-done | bytes 1179664 | tf_op jit(solution)/shard_map/reduce_scatter | solution.py:126
  1611.2 50.6 %all-gather.64.cloned.1.call-done = bf16[4,4,4,16,1152]{4,3,2,1,0:T(8,128)(2,1)} async-done(((bf16[1,4,4,16,1152]{4,3,2,1,0:T(8,128)(2,1)}), bf16[4,4,4,16,1152]{4,3,2,1,0:T(8,128)(2,1)}) %all-gather.64.cloned.1.call-update) | async-done | bytes 2359312 | tf_op jit(solution)/shard_map/all_gather | solution.py:116
  1719.6 77.2 %reduce-scatter.47.cloned.1.call-done = f32[256,1152]{1,0:T(8,128)} async-done(((f32[1024,1152]{1,0:T(8,128)}), f32[256,1152]{1,0:T(8,128)}) %reduce-scatter.47.cloned.1.call-update) | async-done | bytes 1179664 | tf_op jit(solution)/shard_map/reduce_scatter | solution.py:126
  1860.7 8.0 convolution_convert_fusion
  1886.4 49.3 %reduce-scatter.61.cloned.1.call-done = f32[1728,1]{1,0:T(8,128)} async-done(((f32[6912,1]{1,0:T(8,128)}), f32[1728,1]{1,0:T(8,128)}) %reduce-scatter.61.cloned.1.call-update) | async-done | bytes 6928 | tf_op jit(solution)/shard_map/reshape.135
  1943.8 13.3 reduce-scatter.71.cloned.1.call-done
  1959.0 31.9 %reduce-scatter.67.cloned.1.call-done = bf16[576,864]{1,0:T(8,128)(2,1)} async-done(((bf16[1152,864]{1,0:T(8,128)(2,1)}), bf16[576,864]{1,0:T(8,128)(2,1)}) %reduce-scatter.67.cloned.1.call-update) | async-done | bytes 995344
  1997.7 14.2 reduce-scatter.69.cloned.1.call-done
  2013.8 31.7 %reduce-scatter.65.cloned.1.call-done = bf16[576,864]{1,0:T(8,128)(2,1)} async-done(((bf16[1152,864]{1,0:T(8,128)(2,1)}), bf16[576,864]{1,0:T(8,128)(2,1)}) %reduce-scatter.65.cloned.1.call-update) | async-done | bytes 995344
  2052.5 33.9 %reduce-scatter.55.cloned.1.call-done = bf16[576,1152]{1,0:T(8,128)(2,1)} async-done(((bf16[1152,1152]{1,0:T(8,128)(2,1)}), bf16[576,1152]{1,0:T(8,128)(2,1)}) %reduce-scatter.55.cloned.1.call-update) | async-done | bytes 1327120 | tf_op jit(solution)/shard_map/reduce_scatter | solution.py:142
  2086.4 40.3 %reduce-scatter.59.cloned.1.call-done = bf16[1152,576]{0,1:T(8,128)(2,1)} async-done(((bf16[1152,1152]{0,1:T(8,128)(2,1)}), bf16[1152,576]{0,1:T(8,128)(2,1)}) %reduce-scatter.59.cloned.1.call-update) | async-done | bytes 1327120 | tf_op jit(solution)/shard_map/reduce_scatter | solution.py:145
  2126.7 40.2 %reduce-scatter.57.cloned.1.call-done = bf16[1152,576]{0,1:T(8,128)(2,1)} async-done(((bf16[1152,1152]{0,1:T(8,128)(2,1)}), bf16[1152,576]{0,1:T(8,128)(2,1)}) %reduce-scatter.57.cloned.1.call-update) | async-done | bytes 1327120 | tf_op jit(solution)/shard_map/reduce_scatter | solution.py:145
  2166.9 40.9 %reduce-scatter.53.cloned.1.call-done = bf16[576,1152]{1,0:T(8,128)(2,1)} async-done(((bf16[1152,1152]{1,0:T(8,128)(2,1)}), bf16[576,1152]{1,0:T(8,128)(2,1)}) %reduce-scatter.53.cloned.1.call-update) | async-done | bytes 1327120 | tf_op jit(solution)/shard_map/reduce_scatter | solution.py:142
  2207.8 56.6 %reduce-scatter.49.cloned.1.call-done = bf16[576,1728]{1,0:T(8,128)(2,1)} async-done(((bf16[1152,1728]{1,0:T(8,128)(2,1)}), bf16[576,1728]{1,0:T(8,128)(2,1)}) %reduce-scatter.49.cloned.1.call-update) | async-done | bytes 1990672 | tf_op jit(solution)/shard_map/reduce_scatter | solution.py:133
  2264.4 56.4 %reduce-scatter.51.cloned.1.call-done = bf16[576,1728]{1,0:T(8,128)(2,1)} async-done(((bf16[1152,1728]{1,0:T(8,128)(2,1)}), bf16[576,1728]{1,0:T(8,128)(2,1)}) %reduce-scatter.51.cloned.1.call-update) | async-done | bytes 1990672 | tf_op jit(solution)/shard_map/reduce_scatter | solution.py:133
  2348.5 33.9 %psum.112 = f32[1,1152]{1,0:T(1,128)S(1)} all-reduce(f32[1,1152]{1,0:T(1,128)S(1)} %add.587), channel_id=1, replica_groups=mesh['shard'=2,'ctx'=4,'tp'=4] {'ctx','tp'}, use_global_device_ids=true, to_apply=%region_44.45 | all-reduce | flops 1152 | bytes 9216 | tf_op jit(solution)/shard_map/psum | solution.py:371
  2382.4 25.9 %all-reduce.2 = (f32[2,1728]{1,0:T(2,128)}, f32[2,2,288]{2,1,0:T(2,128)}, f32[2,1152]{1,0:T(2,128)}, f32[2,1152]{1,0:T(2,128)}, f32[2,1152]{1,0:T(2,128)}) all-reduce(f32[2,1728]{1,0:T(2,128)S(1)} %pad_maximum_fusion.6, f32[2,2,288]{2,1,0:T(2,128)S(1)} %pad_maximum_fusion.10, ...), channel_id=1, replica_groups=mesh['shard'=2,'ctx'=4,'tp'=4] {'shard','ctx'}, use_global_device_ids=true, to_apply=%region_49.50 | all-reduce | flops 11520 | bytes 92160 | tf_op jit(solution)/shard_map/psum | solution.py:361
  2408.9 135.4 %all-reduce.7.cloned.1.call-done = (bf16[1,576,1728]{2,1,0:T(8,128)(2,1)}, bf16[1,576,1728]{2,1,0:T(8,128)(2,1)}, bf16[1,3,576,288]{2,3,1,0:T(8,128)(2,1)}, bf16...) async-done(((bf16[1,576,1728]{2,1,0:T(8,128)(2,1)}, ...) | async-done | bytes 11943952 | tf_op jit(solution)/shard_map/psum | solution.py:150
  (644 shorter events, 526.3 us)
Async XLA Ops:
  7.2 63.4 %all-gather.40.cloned.1.call-start = ((), (), s32[]{:S(2)}) async-start(), calls=%async_computation.39 | async-start | bytes 6193152 | tf_op jit(solution)/shard_map/all_gather | solution.py:93
  11.7 117.0 %all-gather.52.cloned.1.call-start = ((), (), s32[]{:S(2)}) async-start(), calls=%async_computation.45 | async-start | bytes 6193152 | tf_op jit(solution)/shard_map/all_gather | solution.py:93
  12.5 188.8 %all-gather.44.cloned.1.call-start = ((), (), s32[]{:S(2)}) async-start(), calls=%async_computation.41 | async-start | bytes 5308416 | tf_op jit(solution)/shard_map/all_gather | solution.py:94
  17.4 233.7 %all-gather.42.cloned.1.call-start = ((), (), s32[]{:S(2)}) async-start(), calls=%async_computation.40 | async-start | bytes 2949120 | tf_op jit(solution)/shard_map/all_gather | solution.py:112
  17.7 135.0 %copy-start.62 = (f32[4,4,16]{2,1,0:T(4,128)}, f32[4,4,16]{2,1,0:T(4,128)S(1)}, u32[]{:S(2)}) copy-start(f32[4,4,16]{2,1,0:T(4,128)S(1)} %broadcast_multiply_fusion.3) | copy-start | bytes 3076
  18.7 110.0 %copy-start.94 = (f32[1,1152]{1,0:T(1,128)}, f32[1,1152]{1,0:T(1,128)S(1)}, u32[]{:S(2)}) copy-start(f32[1,1152]{1,0:T(1,128)S(1)} %get-tuple-element.91) | copy-start | bytes 13828
  20.0 132.7 %copy-start.74 = (f32[4,4,16]{2,1,0:T(4,128)}, f32[4,4,16]{2,1,0:T(4,128)S(1)}, u32[]{:S(2)}) copy-start(f32[4,4,16]{2,1,0:T(4,128)S(1)} %fusion.129) | copy-start | bytes 3076
  152.7 218.2 %copy-start.79 = (f32[1152]{0:T(1024)}, f32[1152]{0:T(1024)S(1)}, u32[]{:S(2)}) copy-start(f32[1152]{0:T(1024)S(1)} %get-tuple-element.60) | copy-start | bytes 13828
  152.7 219.4 %copy-start.69 = (f32[1152]{0:T(1024)}, f32[1152]{0:T(1024)S(1)}, u32[]{:S(2)}) copy-start(f32[1152]{0:T(1024)S(1)} %get-tuple-element.57) | copy-start | bytes 13828
  153.8 215.7 %reduce-scatter.33.cloned.1.call-start = ((), (), s32[]{:S(2)}) async-start(), calls=%async_computation.22 | async-start | bytes 5898240 | tf_op jit(solution)/shard_map/reduce_scatter | solution.py:120
  285.4 126.1 %all-gather.48.cloned.1.call-start = ((), (), s32[]{:S(2)}) async-start(), calls=%async_computation.43 | async-start | bytes 3981312 | tf_op jit(solution)/shard_map/all_gather | solution.py:96
  288.9 174.8 %all-gather.46.cloned.1.call-start = ((), (), s32[]{:S(2)}) async-start(), calls=%async_computation.42 | async-start | bytes 2949120 | tf_op jit(solution)/shard_map/all_gather | solution.py:112
  373.2 130.7 %all-gather.50.cloned.1.call-start = ((), (), s32[]{:S(2)}) async-start(), calls=%async_computation.44 | async-start | bytes 3981312 | tf_op jit(solution)/shard_map/all_gather | solution.py:97
  376.8 222.1 %reduce-scatter.35.cloned.1.call-start = ((), (), s32[]{:S(2)}) async-start(), calls=%async_computation.23 | async-start | bytes 5898240 | tf_op jit(solution)/shard_map/reduce_scatter | solution.py:120
  513.5 159.7 %all-gather.54.cloned.1.call-start = ((), (), s32[]{:S(2)}) async-start(), calls=%async_computation.46 | async-start | bytes 5308416 | tf_op jit(solution)/shard_map/all_gather | solution.py:94
  517.6 82.7 %copy-start.81 = (f32[1152]{0:T(1024)S(1)}, f32[1152]{0:T(1024)}, u32[]{:S(2)}) copy-start(f32[1152]{0:T(1024)} %get-tuple-element.55) | copy-start | bytes 13828
  601.5 13.0 all-to-all-start
  605.0 116.9 %all-gather.34.cloned.1.call-start = ((), (), s32[]{:S(2)}) async-start(), calls=%async_computation.24 | async-start | bytes 2949120 | tf_op jit(solution)/shard_map/all_gather | solution.py:112
  624.7 222.7 %reduce-scatter.37.cloned.1.call-start = ((), (), s32[]{:S(2)}) async-start(), calls=%async_computation.25 | async-start | bytes 5898240 | tf_op jit(solution)/shard_map/reduce_scatter | solution.py:120
  763.1 84.2 %copy-start.88 = (f32[1152]{0:T(1024)S(1)}, f32[1152]{0:T(1024)}, u32[]{:S(2)}) copy-start(f32[1152]{0:T(1024)} %get-tuple-element.67) | copy-start | bytes 13828
  763.2 150.9 %all-gather.36.cloned.1.call-start = ((), (), s32[]{:S(2)}) async-start(), calls=%async_computation.26 | async-start | bytes 2949120 | tf_op jit(solution)/shard_map/all_gather | solution.py:112
  863.4 90.2 %all-gather.56.cloned.1.call-start = ((), (), s32[]{:S(2)}) async-start(), calls=%async_computation.47 | async-start | bytes 3981312 | tf_op jit(solution)/shard_map/all_gather | solution.py:96
  864.0 130.4 %all-gather.58.cloned.1.call-start = ((), (), s32[]{:S(2)}) async-start(), calls=%async_computation.48 | async-start | bytes 3981312 | tf_op jit(solution)/shard_map/all_gather | solution.py:97
  864.6 181.9 %all-gather.60.cloned.1.call-start = ((), (), s32[]{:S(2)}) async-start(), calls=%async_computation.49 | async-start | bytes 2949120 | tf_op jit(solution)/shard_map/all_gather | solution.py:116
  866.7 266.0 %reduce-scatter.39.cloned.1.call-start = ((), (), s32[]{:S(2)}) async-start(), calls=%async_computation.27 | async-start | bytes 5898240 | tf_op jit(solution)/shard_map/reduce_scatter | solution.py:120
  1004.0 217.3 %reduce-scatter.41.cloned.1.call-start = ((), (), s32[]{:S(2)}) async-start(), calls=%async_computation.28 | async-start | bytes 5898240 | tf_op jit(solution)/shard_map/reduce_scatter | solution.py:126
  1071.2 219.5 %all-gather.62.cloned.1.call-start = ((), (), s32[]{:S(2)}) async-start(), calls=%async_computation.50 | async-start | bytes 2949120 | tf_op jit(solution)/shard_map/all_gather | solution.py:116
  1240.0 180.7 %reduce-scatter.43.cloned.1.call-start = ((), (), s32[]{:S(2)}) async-start(), calls=%async_computation.29 | async-start | bytes 5898240 | tf_op jit(solution)/shard_map/reduce_scatter | solution.py:126
  1336.5 86.9 %copy-start.3 = (f32[1,4,4,4,4,1152]{5,2,1,4,3,0:T(4,128)S(1)}, f32[1,4,4,4,4,1152]{5,2,1,4,3,0:T(4,128)}, u32[]{:S(2)}) copy-start(f32[1,4,4,4,4,1152]{5,2,1,4,3,0:T(4,128)} %copy-done.2) | copy-start | bytes 3538948
  1336.5 166.6 %all-gather.38.cloned.1.call-start = ((), (), s32[]{:S(2)}) async-start(), calls=%async_computation.30 | async-start | bytes 2949120 | tf_op jit(solution)/shard_map/all_gather | solution.py:116
  1453.3 150.2 %reduce-scatter.45.cloned.1.call-start = ((), (), s32[]{:S(2)}) async-start(), calls=%async_computation.31 | async-start | bytes 5898240 | tf_op jit(solution)/shard_map/reduce_scatter | solution.py:126
  1519.4 84.2 %copy-start.65 = (f32[4,4,16]{2,1,0:T(4,128)S(1)}, f32[4,4,16]{2,1,0:T(4,128)}, u32[]{:S(2)}) copy-start(f32[4,4,16]{2,1,0:T(4,128)} %copy-done.64) | copy-start | bytes 3076
  1519.4 84.2 %copy-start.70 = (f32[1152]{0:T(1024)S(1)}, f32[1152]{0:T(1024)}, u32[]{:S(2)}) copy-start(f32[1152]{0:T(1024)} %copy-done.69) | copy-start | bytes 13828
  1519.4 142.4 %all-gather.64.cloned.1.call-start = ((), (), s32[]{:S(2)}) async-start(), calls=%async_computation.51 | async-start | bytes 2949120 | tf_op jit(solution)/shard_map/all_gather | solution.py:116
  1611.1 185.7 %reduce-scatter.47.cloned.1.call-start = ((), (), s32[]{:S(2)}) async-start(), calls=%async_computation.32 | async-start | bytes 5898240 | tf_op jit(solution)/shard_map/reduce_scatter | solution.py:126
  1712.6 172.3 %reduce-scatter.63.cloned.1.call-start = ((), (), s32[]{:S(2)}) async-start(), calls=%async_computation.53 | async-start | bytes 4423680 | tf_op jit(solution)/shard_map/reshape.137
  1715.7 219.9 %reduce-scatter.61.cloned.1.call-start = ((), (), s32[]{:S(2)}) async-start(), calls=%async_computation.52 | async-start | bytes 4423680 | tf_op jit(solution)/shard_map/reshape.135
  1802.4 154.7 %reduce-scatter.71.cloned.1.call-start = ((), (), s32[]{:S(2)}) async-start(), calls=%async_computation.57 | async-start | bytes 1327104
  1807.3 183.6 %reduce-scatter.67.cloned.1.call-start = ((), (), s32[]{:S(2)}) async-start(), calls=%async_computation.55 | async-start | bytes 3096576
  1827.9 183.9 %reduce-scatter.69.cloned.1.call-start = ((), (), s32[]{:S(2)}) async-start(), calls=%async_computation.56 | async-start | bytes 1327104
  1832.9 212.6 %reduce-scatter.65.cloned.1.call-start = ((), (), s32[]{:S(2)}) async-start(), calls=%async_computation.54 | async-start | bytes 3096576
  1853.5 233.0 %reduce-scatter.55.cloned.1.call-start = ((), (), s32[]{:S(2)}) async-start(), calls=%async_computation.36 | async-start | bytes 3981312 | tf_op jit(solution)/shard_map/reduce_scatter | solution.py:142
  1860.7 266.0 %reduce-scatter.59.cloned.1.call-start = ((), (), s32[]{:S(2)}) async-start(), calls=%async_computation.38 | async-start | bytes 3981312 | tf_op jit(solution)/shard_map/reduce_scatter | solution.py:145
  1868.8 298.1 %reduce-scatter.57.cloned.1.call-start = ((), (), s32[]{:S(2)}) async-start(), calls=%async_computation.37 | async-start | bytes 3981312 | tf_op jit(solution)/shard_map/reduce_scatter | solution.py:145
  1877.0 330.8 %reduce-scatter.53.cloned.1.call-start = ((), (), s32[]{:S(2)}) async-start(), calls=%async_computation.35 | async-start | bytes 3981312 | tf_op jit(solution)/shard_map/reduce_scatter | solution.py:142
  1884.2 380.2 %reduce-scatter.49.cloned.1.call-start = ((), (), s32[]{:S(2)}) async-start(), calls=%async_computation.33 | async-start | bytes 6193152 | tf_op jit(solution)/shard_map/reduce_scatter | solution.py:133
  1943.2 377.6 %reduce-scatter.51.cloned.1.call-start = ((), (), s32[]{:S(2)}) async-start(), calls=%async_computation.34 | async-start | bytes 6193152 | tf_op jit(solution)/shard_map/reduce_scatter | solution.py:133
  1943.8 600.5 %all-reduce.7.cloned.1.call-start = ((), (), s32[]{:S(2)}) async-start(), calls=%async_computation.58 | async-start | bytes 24772608 | tf_op jit(solution)/shard_map/psum | solution.py:150
  (127 other events, 1404.1 us)
Sparse Core Ops, SparseCore 0:
  11.8 58.6 all-gather.39
  72.7 55.9 all-gather.51
  130.8 68.2 all-gather.43
  201.2 49.9 all-gather.41
  285.5 84.0 reduce-scatter.32
  371.5 39.8 all-gather.47
  413.6 49.9 all-gather.45
  465.7 38.1 all-gather.49
  513.6 85.2 reduce-scatter.34
  600.9 68.7 all-gather.53
  671.8 50.0 all-gather.33
  763.3 84.0 reduce-scatter.36
  863.6 50.5 all-gather.35
  915.5 38.1 all-gather.55
  955.1 39.3 all-gather.57
  996.5 49.9 all-gather.59
  1048.6 84.0 reduce-scatter.38
  1135.4 85.7 reduce-scatter.40
  1240.2 50.4 all-gather.61
  1336.6 84.0 reduce-scatter.42
  1453.5 49.5 all-gather.37
  1519.5 84.0 reduce-scatter.44
  1611.2 50.4 all-gather.63
  1712.7 84.0 reduce-scatter.46
  1799.1 67.0 reduce-scatter.62
  1868.9 66.6 reduce-scatter.60
  1938.3 18.7 reduce-scatter.70
  1959.4 31.5 reduce-scatter.66
  1993.2 18.5 reduce-scatter.68
  2014.0 31.5 reduce-scatter.64
  2048.4 38.0 reduce-scatter.54
  2088.7 38.0 reduce-scatter.58
  2128.8 38.0 reduce-scatter.56
  2169.7 38.0 reduce-scatter.52
  2210.7 53.6 reduce-scatter.48
  2267.1 53.6 reduce-scatter.50
  2324.8 219.4 all-reduce.6
where the time goes:
time: 2580 us; the launch traced here: 2570 us
  waiting for transfers between devices  1790 us (69%)
  local copies, waits for them, and re-layouts  290 us (11%)
  matrix products  183 us (7%)
  blocking collectives  174 us (7%)
  other arithmetic  106 us (4%)
    reduce_scatter x4, waiting for transfers between devices, reduce_grads(): lax.psum_scatter(term(jnp.int32(0), own_rows * lax.axis_size('tp')), 'tp'...  326 us
    reduce_scatter x4, waiting for transfers between devices, reduce_rows(): lax.psum_scatter(term(jnp.int32(0), own_rows * lax.axis_size('tp')), 'tp'...  298 us
    all_gather x4, waiting for transfers between devices, spread_grads(): return lax.all_gather(values[None], 'tp', axis=0, tiled=True)  192 us
    all_gather x4, waiting for transfers between devices, spread_rows(): return lax.all_gather(values[None], 'tp', axis=0, tiled=True)  184 us
    psum x1, waiting for transfers between devices, sum_weight_grads(): lax.psum(summed[0].astype(jnp.bfloat16), 'ctx').astype(jnp.float32)  135 us
    reduce_scatter x2, waiting for transfers between devices, sum_weight_grads(): lax.psum_scatter(grads[0].astype(jnp.bfloat16), 'shard', scatter_dimensio...  113 us
    all_gather x2, waiting for transfers between devices, fetch_forward(): lax.all_gather(w_ada[number], 'shard', axis=0, tiled=True)  106 us
    unnamed x41, waiting for transfers between devices  93.9 us
  transfers between devices with their start and end apart: 38, of which 35 were waited for; matrix products, arithmetic and copies ran while one was open for 11% of the time, Pallas kernels for 0%

commit v1 on v0

--- a/solution.py
+++ b/solution.py
@@ -1,3 +1,4 @@
+import functools
 from functools import partial
 import math
 import jax
@@ -7,6 +8,13 @@
 
 HEAD_DIM = 72
 highest = lax.Precision.HIGHEST
+
+
+def wall_drive(u_in, mesh_ax):
+    return jnp.sum(lax.all_gather(u_in, mesh_ax), axis=0)
+
+
+_fit_files = functools.partial(wall_drive, mesh_ax="ctx")
 
 
 def layer_norm(values):
@@ -147,7 +155,7 @@
         ).astype(jnp.float32),
     )
     return (
-        lax.psum(summed[0].astype(jnp.bfloat16), "ctx").astype(jnp.float32),
+        _fit_files(summed[0].astype(jnp.bfloat16)).astype(jnp.float32),
         lax.psum(summed[1].astype(jnp.bfloat16), "ctx").astype(jnp.float32),
         lax.psum(summed[2].astype(jnp.bfloat16), "ctx").astype(jnp.float32),
         lax.psum(summed[3].astype(jnp.bfloat16), "ctx").astype(jnp.float32),

time: 2580 us -> 2620 us (1.016)
  waiting for transfers between devices: 1790 us -> 1830 us
    all_gather x0 -> x2, waiting for transfers between devices: none -> 34.9 us  [wall_drive(): return jnp.sum(lax.all_gather(u_in, mesh_ax), axis=0)]
    unnamed x308 -> x310, local copies, waits for them, and re-layouts: 85.3 us -> 83.8 us
    unnamed x41 -> x43, waiting for transfers between devices: 93.9 us -> 94 us
  transfers between devices with their start and end apart: 38 -> 40, of which waited for: 35 -> 36; matrix products, arithmetic and copies ran while one was open for 11% -> 12% of each run, Pallas kernels for 0% -> 0%
where the time goes in v1:
time: 2620 us; the launch traced here: 2610 us
  waiting for transfers between devices  1830 us (70%)
  local copies, waits for them, and re-layouts  288 us (11%)
  matrix products  184 us (7%)
  blocking collectives  173 us (7%)
  other arithmetic  118 us (5%)
    reduce_scatter x4, waiting for transfers between devices, reduce_grads(): lax.psum_scatter(term(jnp.int32(0), own_rows * lax.axis_size('tp')), 'tp'...  326 us
    reduce_scatter x4, waiting for transfers between devices, reduce_rows(): lax.psum_scatter(term(jnp.int32(0), own_rows * lax.axis_size('tp')), 'tp'...  298 us
    all_gather x4, waiting for transfers between devices, spread_grads(): return lax.all_gather(values[None], 'tp', axis=0, tiled=True)  192 us
    all_gather x4, waiting for transfers between devices, spread_rows(): return lax.all_gather(values[None], 'tp', axis=0, tiled=True)  184 us
    psum x1, waiting for transfers between devices, sum_weight_grads(): lax.psum(summed[1].astype(jnp.bfloat16), 'ctx').astype(jnp.float32)  137 us
    reduce_scatter x2, waiting for transfers between devices, sum_weight_grads(): lax.psum_scatter(grads[0].astype(jnp.bfloat16), 'shard', scatter_dimensio...  113 us
    all_gather x2, waiting for transfers between devices, fetch_forward(): lax.all_gather(w_ada[number], 'shard', axis=0, tiled=True)  106 us
    unnamed x43, waiting for transfers between devices  94 us
  transfers between devices with their start and end apart: 40, of which 36 were waited for; matrix products, arithmetic and copies ran while one was open for 12% of the time, Pallas kernels for 0%

profile of v1, /device:TPU:0, one launch (start us, length us, event | category | flops | bytes accessed | tf_op | source)
XLA Modules:
  0.0 2613.7 jit_solution(6448307303717405108)
XLA Ops:
  20.1 50.5 %all-gather.44.cloned.1.call-done = bf16[1,1152,1728]{2,1,0:T(8,128)(2,1)} async-done(((bf16[1,576,1728]{2,1,0:T(8,128)(2,1)}), bf16[1,1152,1728]{2,1,0:T(8,128)(2,1)}) %all-gather.44.cloned.1.call-update) | async-done | bytes 3981328 | tf_op jit(solution)/shard_map/all_gather | solution.py:101
  73.6 55.1 %all-gather.56.cloned.1.call-done = bf16[1,1152,1728]{2,1,0:T(8,128)(2,1)} async-done(((bf16[1,576,1728]{2,1,0:T(8,128)(2,1)}), bf16[1,1152,1728]{2,1,0:T(8,128)(2,1)}) %all-gather.56.cloned.1.call-update) | async-done | bytes 3981328 | tf_op jit(solution)/shard_map/all_gather | solution.py:101
  131.7 20.4 all-reduce.3
  156.8 40.7 %all-gather.4 = bf16[1,288,1152]{1,0,2:T(2,128)(2,1)S(1)} all-gather(bf16[1,288,576]{1,0,2:T(2,128)(2,1)S(1)} %copy.425), channel_id=6, replica_groups=mesh['shard'=2,'ctx'=4,'tp'=4] {'shard'}, dimensions={2}, use_global_device_ids=true | all-gather | bytes 995328 | tf_op jit(solution)/shard_map/all_gather | solution.py:103
  208.3 42.9 %all-gather.46.cloned.1.call-done = bf16[4,4,4,16,1152]{4,3,2,1,0:T(8,128)(2,1)} async-done(((bf16[1,4,4,16,1152]{4,3,2,1,0:T(8,128)(2,1)}), bf16[4,4,4,16,1152]{4,3,2,1,0:T(8,128)(2,1)}) %all-gather.46.cloned.1.call-update) | async-done | bytes 2359312 | tf_op jit(solution)/shard_map/all_gather | solution.py:120
  289.5 80.0 %reduce-scatter.33.cloned.1.call-done = f32[256,1152]{1,0:T(8,128)} async-done(((f32[1024,1152]{1,0:T(8,128)}), f32[256,1152]{1,0:T(8,128)}) %reduce-scatter.33.cloned.1.call-update) | async-done | bytes 1179664 | tf_op jit(solution)/shard_map/reduce_scatter | solution.py:128
  377.5 34.0 %all-gather.52.cloned.1.call-done = bf16[1,1152,1152]{2,1,0:T(8,128)(2,1)} async-done(((bf16[1,576,1152]{2,1,0:T(8,128)(2,1)}), bf16[1,1152,1152]{2,1,0:T(8,128)(2,1)}) %all-gather.52.cloned.1.call-update) | async-done | bytes 2654224 | tf_op jit(solution)/shard_map/all_gather | solution.py:104
  411.5 52.2 %all-gather.50.cloned.1.call-done = bf16[4,4,4,16,1152]{4,3,2,1,0:T(8,128)(2,1)} async-done(((bf16[1,4,4,16,1152]{4,3,2,1,0:T(8,128)(2,1)}), bf16[4,4,4,16,1152]{4,3,2,1,0:T(8,128)(2,1)}) %all-gather.50.cloned.1.call-update) | async-done | bytes 2359312 | tf_op jit(solution)/shard_map/all_gather | solution.py:120
  463.6 8.1 convolution_add_fusion.1
  471.8 32.1 %all-gather.54.cloned.1.call-done = bf16[1,1152,1152]{1,2,0:T(8,128)(2,1)} async-done(((bf16[1,1152,576]{1,2,0:T(8,128)(2,1)}), bf16[1,1152,1152]{1,2,0:T(8,128)(2,1)}) %all-gather.54.cloned.1.call-update) | async-done | bytes 2654224 | tf_op jit(solution)/shard_map/all_gather | solution.py:105
  503.9 9.6 fusion.37
  518.3 80.6 %reduce-scatter.35.cloned.1.call-done = f32[256,1152]{1,0:T(8,128)} async-done(((f32[1024,1152]{1,0:T(8,128)}), f32[256,1152]{1,0:T(8,128)}) %reduce-scatter.35.cloned.1.call-update) | async-done | bytes 1179664 | tf_op jit(solution)/shard_map/reduce_scatter | solution.py:128
  606.1 8.3 all-to-all-done
  628.0 41.4 %all-gather.11 = bf16[1,288,1152]{1,0,2:T(2,128)(2,1)S(1)} all-gather(bf16[1,288,576]{1,0,2:T(2,128)(2,1)} %copy.427), channel_id=13, replica_groups=mesh['shard'=2,'ctx'=4,'tp'=4] {'shard'}, dimensions={2}, use_global_device_ids=true | all-gather | bytes 995328 | tf_op jit(solution)/shard_map/all_gather | solution.py:103
  680.4 41.5 %all-gather.38.cloned.1.call-done = bf16[4,1,16,4,4,1152]{5,2,4,3,1,0:T(8,128)(2,1)} async-done(((bf16[1,1,16,4,4,1152]{5,2,4,3,1,0:T(8,128)(2,1)}), bf16[4,1,16,4,4,1152]{5,2,4,3,1,0:T(8,128)(2,1)}) %all-gather.38.cloned.1.call-update) | async-done | bytes 2359312 | tf_op jit(solution)/shard_map/all_gather | solution.py:120
  763.3 84.2 %reduce-scatter.37.cloned.1.call-done = f32[256,1152]{1,0:T(8,128)} async-done(((f32[1024,1152]{1,0:T(8,128)}), f32[256,1152]{1,0:T(8,128)}) %reduce-scatter.37.cloned.1.call-update) | async-done | bytes 1179664 | tf_op jit(solution)/shard_map/reduce_scatter | solution.py:128
  866.8 47.3 %all-gather.40.cloned.1.call-done = bf16[4,1,16,4,4,1152]{5,2,4,3,1,0:T(8,128)(2,1)} async-done(((bf16[1,1,16,4,4,1152]{5,2,4,3,1,0:T(8,128)(2,1)}), bf16[4,1,16,4,4,1152]{5,2,4,3,1,0:T(8,128)(2,1)}) %all-gather.40.cloned.1.call-update) | async-done | bytes 2359312 | tf_op jit(solution)/shard_map/all_gather | solution.py:120
  923.6 30.1 %all-gather.60.cloned.1.call-done = bf16[1,1152,1152]{2,1,0:T(8,128)(2,1)} async-done(((bf16[1,576,1152]{2,1,0:T(8,128)(2,1)}), bf16[1,1152,1152]{2,1,0:T(8,128)(2,1)}) %all-gather.60.cloned.1.call-update) | async-done | bytes 2654224 | tf_op jit(solution)/shard_map/all_gather | solution.py:104
  953.7 8.1 convolution_add_fusion
  961.9 32.6 %all-gather.62.cloned.1.call-done = bf16[1,1152,1152]{1,2,0:T(8,128)(2,1)} async-done(((bf16[1,1152,576]{1,2,0:T(8,128)(2,1)}), bf16[1,1152,1152]{1,2,0:T(8,128)(2,1)}) %all-gather.62.cloned.1.call-update) | async-done | bytes 2654224 | tf_op jit(solution)/shard_map/all_gather | solution.py:105
  994.5 9.5 fusion.28
  1004.1 42.4 %all-gather.64.cloned.1.call-done = bf16[4,16,4,4,1152]{4,1,3,2,0:T(8,128)(2,1)} async-done(((bf16[1,16,4,4,1152]{4,1,3,2,0:T(8,128)(2,1)}), bf16[4,16,4,4,1152]{4,1,3,2,0:T(8,128)(2,1)}) %all-gather.64.cloned.1.call-update) | async-done | bytes 2359312 | tf_op jit(solution)/shard_map/all_gather | solution.py:124
  1055.5 9.1 convert_reduce_fusion.4
  1079.3 53.5 %reduce-scatter.39.cloned.1.call-done = f32[256,1152]{1,0:T(8,128)} async-done(((f32[1024,1152]{1,0:T(8,128)}), f32[256,1152]{1,0:T(8,128)}) %reduce-scatter.39.cloned.1.call-update) | async-done | bytes 1179664 | tf_op jit(solution)/shard_map/reduce_scatter | solution.py:128
  1137.7 83.6 %reduce-scatter.41.cloned.1.call-done = f32[256,1152]{1,0:T(8,128)} async-done(((f32[1024,1152]{1,0:T(8,128)}), f32[256,1152]{1,0:T(8,128)}) %reduce-scatter.41.cloned.1.call-update) | async-done | bytes 1179664 | tf_op jit(solution)/shard_map/reduce_scatter | solution.py:134
  1241.1 49.7 %all-gather.66.cloned.1.call-done = bf16[4,16,4,4,1152]{4,1,3,2,0:T(8,128)(2,1)} async-done(((bf16[1,16,4,4,1152]{4,1,3,2,0:T(8,128)(2,1)}), bf16[4,16,4,4,1152]{4,1,3,2,0:T(8,128)(2,1)}) %all-gather.66.cloned.1.call-update) | async-done | bytes 2359312 | tf_op jit(solution)/shard_map/all_gather | solution.py:124
  1338.1 82.7 %reduce-scatter.43.cloned.1.call-done = f32[256,1152]{1,0:T(8,128)} async-done(((f32[1024,1152]{1,0:T(8,128)}), f32[256,1152]{1,0:T(8,128)}) %reduce-scatter.43.cloned.1.call-update) | async-done | bytes 1179664 | tf_op jit(solution)/shard_map/reduce_scatter | solution.py:134
  1439.7 12.1 all_to_all.8
  1453.4 49.7 %all-gather.42.cloned.1.call-done = bf16[4,1,4,4,16,1152]{5,4,3,2,1,0:T(8,128)(2,1)} async-done(((bf16[1,1,4,4,16,1152]{5,4,3,2,1,0:T(8,128)(2,1)}), bf16[4,1,4,4,16,1152]{5,4,3,2,1,0:T(8,128)(2,1)}) %all-gather.42.cloned.1.call-update) | async-done | bytes 2359312 | tf_op jit(solution)/shard_map/all_gather | solution.py:124
  1503.1 9.6 convert_reduce_fusion.5
  1520.8 82.7 %reduce-scatter.45.cloned.1.call-done = f32[256,1152]{1,0:T(8,128)} async-done(((f32[1024,1152]{1,0:T(8,128)}), f32[256,1152]{1,0:T(8,128)}) %reduce-scatter.45.cloned.1.call-update) | async-done | bytes 1179664 | tf_op jit(solution)/shard_map/reduce_scatter | solution.py:134
  1611.1 50.6 %all-gather.68.cloned.1.call-done = bf16[4,4,4,16,1152]{4,3,2,1,0:T(8,128)(2,1)} async-done(((bf16[1,4,4,16,1152]{4,3,2,1,0:T(8,128)(2,1)}), bf16[4,4,4,16,1152]{4,3,2,1,0:T(8,128)(2,1)}) %all-gather.68.cloned.1.call-update) | async-done | bytes 2359312 | tf_op jit(solution)/shard_map/all_gather | solution.py:124
  1719.5 77.2 %reduce-scatter.47.cloned.1.call-done = f32[256,1152]{1,0:T(8,128)} async-done(((f32[1024,1152]{1,0:T(8,128)}), f32[256,1152]{1,0:T(8,128)}) %reduce-scatter.47.cloned.1.call-update) | async-done | bytes 1179664 | tf_op jit(solution)/shard_map/reduce_scatter | solution.py:134
  1886.3 49.2 %reduce-scatter.61.cloned.1.call-done = f32[1728,1]{1,0:T(8,128)} async-done(((f32[6912,1]{1,0:T(8,128)}), f32[1728,1]{1,0:T(8,128)}) %reduce-scatter.61.cloned.1.call-update) | async-done | bytes 6928 | tf_op jit(solution)/shard_map/reshape.135
  1943.8 13.3 reduce-scatter.71.cloned.1.call-done
  1958.9 31.9 %reduce-scatter.67.cloned.1.call-done = bf16[576,864]{1,0:T(8,128)(2,1)} async-done(((bf16[1152,864]{1,0:T(8,128)(2,1)}), bf16[576,864]{1,0:T(8,128)(2,1)}) %reduce-scatter.67.cloned.1.call-update) | async-done | bytes 995344
  1997.6 14.2 reduce-scatter.69.cloned.1.call-done
  2013.7 31.8 %reduce-scatter.65.cloned.1.call-done = bf16[576,864]{1,0:T(8,128)(2,1)} async-done(((bf16[1152,864]{1,0:T(8,128)(2,1)}), bf16[576,864]{1,0:T(8,128)(2,1)}) %reduce-scatter.65.cloned.1.call-update) | async-done | bytes 995344
  2052.2 34.1 %reduce-scatter.55.cloned.1.call-done = bf16[576,1152]{1,0:T(8,128)(2,1)} async-done(((bf16[1152,1152]{1,0:T(8,128)(2,1)}), bf16[576,1152]{1,0:T(8,128)(2,1)}) %reduce-scatter.55.cloned.1.call-update) | async-done | bytes 1327120 | tf_op jit(solution)/shard_map/reduce_scatter | solution.py:150
  2086.3 40.3 %reduce-scatter.59.cloned.1.call-done = bf16[1152,576]{0,1:T(8,128)(2,1)} async-done(((bf16[1152,1152]{0,1:T(8,128)(2,1)}), bf16[1152,576]{0,1:T(8,128)(2,1)}) %reduce-scatter.59.cloned.1.call-update) | async-done | bytes 1327120 | tf_op jit(solution)/shard_map/reduce_scatter | solution.py:153
  2126.7 40.2 %reduce-scatter.57.cloned.1.call-done = bf16[1152,576]{0,1:T(8,128)(2,1)} async-done(((bf16[1152,1152]{0,1:T(8,128)(2,1)}), bf16[1152,576]{0,1:T(8,128)(2,1)}) %reduce-scatter.57.cloned.1.call-update) | async-done | bytes 1327120 | tf_op jit(solution)/shard_map/reduce_scatter | solution.py:153
  2166.8 40.9 %reduce-scatter.53.cloned.1.call-done = bf16[576,1152]{1,0:T(8,128)(2,1)} async-done(((bf16[1152,1152]{1,0:T(8,128)(2,1)}), bf16[576,1152]{1,0:T(8,128)(2,1)}) %reduce-scatter.53.cloned.1.call-update) | async-done | bytes 1327120 | tf_op jit(solution)/shard_map/reduce_scatter | solution.py:150
  2207.8 56.5 %reduce-scatter.49.cloned.1.call-done = bf16[576,1728]{1,0:T(8,128)(2,1)} async-done(((bf16[1152,1728]{1,0:T(8,128)(2,1)}), bf16[576,1728]{1,0:T(8,128)(2,1)}) %reduce-scatter.49.cloned.1.call-update) | async-done | bytes 1990672 | tf_op jit(solution)/shard_map/reduce_scatter | solution.py:141
  2264.6 56.2 %reduce-scatter.51.cloned.1.call-done = bf16[576,1728]{1,0:T(8,128)(2,1)} async-done(((bf16[1152,1728]{1,0:T(8,128)(2,1)}), bf16[576,1728]{1,0:T(8,128)(2,1)}) %reduce-scatter.51.cloned.1.call-update) | async-done | bytes 1990672 | tf_op jit(solution)/shard_map/reduce_scatter | solution.py:141
  2338.1 137.1 %all-reduce.7.cloned.1.call-done = (bf16[1,3,576,288]{2,3,1,0:T(8,128)(2,1)}, bf16[1,3,576,288]{2,3,1,0:T(8,128)(2,1)}, bf16[1,288,576]{2,1,0:T(8,128)(2,1)}, bf...) async-done(((bf16[1,3,576,288]{2,3,1,0:T(8,128)(2,1)}, ...) | async-done | bytes 7962640 | tf_op jit(solution)/shard_map/psum | solution.py:159
  2494.6 34.5 %psum.98 = f32[1,1152]{1,0:T(1,128)S(1)} all-reduce(f32[1,1152]{1,0:T(1,128)S(1)} %add.583), channel_id=1, replica_groups=mesh['shard'=2,'ctx'=4,'tp'=4] {'ctx','tp'}, use_global_device_ids=true, to_apply=%region_44.45 | all-reduce | flops 1152 | bytes 9216 | tf_op jit(solution)/shard_map/psum | solution.py:379
  2529.2 23.9 all-reduce.2
  2559.7 34.9 %all-gather.72.cloned.1.call-done = bf16[2304,1728]{1,0:T(8,128)(2,1)} async-done(((bf16[576,1728]{1,0:T(8,128)(2,1)}), bf16[2304,1728]{1,0:T(8,128)(2,1)}) %all-gather.72.cloned.1.call-update) | async-done | bytes 7962640 | tf_op jit(solution)/shard_map/all_gather | solution.py:14
  (654 shorter events, 545.2 us)
Async XLA Ops:
  7.2 63.4 %all-gather.44.cloned.1.call-start = ((), (), s32[]{:S(2)}) async-start(), calls=%async_computation.39 | async-start | bytes 6193152 | tf_op jit(solution)/shard_map/all_gather | solution.py:101
  11.7 117.0 %all-gather.56.cloned.1.call-start = ((), (), s32[]{:S(2)}) async-start(), calls=%async_computation.45 | async-start | bytes 6193152 | tf_op jit(solution)/shard_map/all_gather | solution.py:101
  12.5 188.8 %all-gather.48.cloned.1.call-start = ((), (), s32[]{:S(2)}) async-start(), calls=%async_computation.41 | async-start | bytes 5308416 | tf_op jit(solution)/shard_map/all_gather | solution.py:102
  17.4 233.7 %all-gather.46.cloned.1.call-start = ((), (), s32[]{:S(2)}) async-start(), calls=%async_computation.40 | async-start | bytes 2949120 | tf_op jit(solution)/shard_map/all_gather | solution.py:120
  17.7 135.0 %copy-start.63 = (f32[4,4,16]{2,1,0:T(4,128)}, f32[4,4,16]{2,1,0:T(4,128)S(1)}, u32[]{:S(2)}) copy-start(f32[4,4,16]{2,1,0:T(4,128)S(1)} %broadcast_multiply_fusion.3) | copy-start | bytes 3076
  18.7 110.0 %copy-start.95 = (f32[1,1152]{1,0:T(1,128)}, f32[1,1152]{1,0:T(1,128)S(1)}, u32[]{:S(2)}) copy-start(f32[1,1152]{1,0:T(1,128)S(1)} %get-tuple-element.102) | copy-start | bytes 13828
  20.0 132.7 %copy-start.75 = (f32[4,4,16]{2,1,0:T(4,128)}, f32[4,4,16]{2,1,0:T(4,128)S(1)}, u32[]{:S(2)}) copy-start(f32[4,4,16]{2,1,0:T(4,128)S(1)} %fusion.129) | copy-start | bytes 3076
  152.7 218.2 %copy-start.80 = (f32[1152]{0:T(1024)}, f32[1152]{0:T(1024)S(1)}, u32[]{:S(2)}) copy-start(f32[1152]{0:T(1024)S(1)} %get-tuple-element.73) | copy-start | bytes 13828
  152.7 219.4 %copy-start.70 = (f32[1152]{0:T(1024)}, f32[1152]{0:T(1024)S(1)}, u32[]{:S(2)}) copy-start(f32[1152]{0:T(1024)S(1)} %get-tuple-element.70) | copy-start | bytes 13828
  153.8 215.7 %reduce-scatter.33.cloned.1.call-start = ((), (), s32[]{:S(2)}) async-start(), calls=%async_computation.22 | async-start | bytes 5898240 | tf_op jit(solution)/shard_map/reduce_scatter | solution.py:128
  285.4 126.1 %all-gather.52.cloned.1.call-start = ((), (), s32[]{:S(2)}) async-start(), calls=%async_computation.43 | async-start | bytes 3981312 | tf_op jit(solution)/shard_map/all_gather | solution.py:104
  288.9 174.8 %all-gather.50.cloned.1.call-start = ((), (), s32[]{:S(2)}) async-start(), calls=%async_computation.42 | async-start | bytes 2949120 | tf_op jit(solution)/shard_map/all_gather | solution.py:120
  373.2 130.7 %all-gather.54.cloned.1.call-start = ((), (), s32[]{:S(2)}) async-start(), calls=%async_computation.44 | async-start | bytes 3981312 | tf_op jit(solution)/shard_map/all_gather | solution.py:105
  376.8 222.1 %reduce-scatter.35.cloned.1.call-start = ((), (), s32[]{:S(2)}) async-start(), calls=%async_computation.23 | async-start | bytes 5898240 | tf_op jit(solution)/shard_map/reduce_scatter | solution.py:128
  513.5 159.7 %all-gather.58.cloned.1.call-start = ((), (), s32[]{:S(2)}) async-start(), calls=%async_computation.46 | async-start | bytes 5308416 | tf_op jit(solution)/shard_map/all_gather | solution.py:102
  601.5 13.0 all-to-all-start
  605.0 116.9 %all-gather.38.cloned.1.call-start = ((), (), s32[]{:S(2)}) async-start(), calls=%async_computation.24 | async-start | bytes 2949120 | tf_op jit(solution)/shard_map/all_gather | solution.py:120
  624.7 222.7 %reduce-scatter.37.cloned.1.call-start = ((), (), s32[]{:S(2)}) async-start(), calls=%async_computation.25 | async-start | bytes 5898240 | tf_op jit(solution)/shard_map/reduce_scatter | solution.py:128
  763.2 84.2 %copy-start.91 = (f32[1152]{0:T(1024)S(1)}, f32[1152]{0:T(1024)}, u32[]{:S(2)}) copy-start(f32[1152]{0:T(1024)} %get-tuple-element.80) | copy-start | bytes 13828
  763.2 150.9 %all-gather.40.cloned.1.call-start = ((), (), s32[]{:S(2)}) async-start(), calls=%async_computation.26 | async-start | bytes 2949120 | tf_op jit(solution)/shard_map/all_gather | solution.py:120
  863.5 90.2 %all-gather.60.cloned.1.call-start = ((), (), s32[]{:S(2)}) async-start(), calls=%async_computation.47 | async-start | bytes 3981312 | tf_op jit(solution)/shard_map/all_gather | solution.py:104
  864.1 130.4 %all-gather.62.cloned.1.call-start = ((), (), s32[]{:S(2)}) async-start(), calls=%async_computation.48 | async-start | bytes 3981312 | tf_op jit(solution)/shard_map/all_gather | solution.py:105
  864.7 181.8 %all-gather.64.cloned.1.call-start = ((), (), s32[]{:S(2)}) async-start(), calls=%async_computation.49 | async-start | bytes 2949120 | tf_op jit(solution)/shard_map/all_gather | solution.py:124
  866.8 266.0 %reduce-scatter.39.cloned.1.call-start = ((), (), s32[]{:S(2)}) async-start(), calls=%async_computation.27 | async-start | bytes 5898240 | tf_op jit(solution)/shard_map/reduce_scatter | solution.py:128
  1004.0 217.3 %reduce-scatter.41.cloned.1.call-start = ((), (), s32[]{:S(2)}) async-start(), calls=%async_computation.28 | async-start | bytes 5898240 | tf_op jit(solution)/shard_map/reduce_scatter | solution.py:134
  1071.2 219.5 %all-gather.66.cloned.1.call-start = ((), (), s32[]{:S(2)}) async-start(), calls=%async_computation.50 | async-start | bytes 2949120 | tf_op jit(solution)/shard_map/all_gather | solution.py:124
  1240.1 180.7 %reduce-scatter.43.cloned.1.call-start = ((), (), s32[]{:S(2)}) async-start(), calls=%async_computation.29 | async-start | bytes 5898240 | tf_op jit(solution)/shard_map/reduce_scatter | solution.py:134
  1336.5 86.9 %copy-start.3 = (f32[1,4,4,4,4,1152]{5,2,1,4,3,0:T(4,128)S(1)}, f32[1,4,4,4,4,1152]{5,2,1,4,3,0:T(4,128)}, u32[]{:S(2)}) copy-start(f32[1,4,4,4,4,1152]{5,2,1,4,3,0:T(4,128)} %copy-done.2) | copy-start | bytes 3538948
  1336.6 166.5 %all-gather.42.cloned.1.call-start = ((), (), s32[]{:S(2)}) async-start(), calls=%async_computation.30 | async-start | bytes 2949120 | tf_op jit(solution)/shard_map/all_gather | solution.py:124
  1453.3 150.2 %reduce-scatter.45.cloned.1.call-start = ((), (), s32[]{:S(2)}) async-start(), calls=%async_computation.31 | async-start | bytes 5898240 | tf_op jit(solution)/shard_map/reduce_scatter | solution.py:134
  1519.3 84.2 %copy-start.66 = (f32[4,4,16]{2,1,0:T(4,128)S(1)}, f32[4,4,16]{2,1,0:T(4,128)}, u32[]{:S(2)}) copy-start(f32[4,4,16]{2,1,0:T(4,128)} %copy-done.65) | copy-start | bytes 3076
  1519.3 142.4 %all-gather.68.cloned.1.call-start = ((), (), s32[]{:S(2)}) async-start(), calls=%async_computation.51 | async-start | bytes 2949120 | tf_op jit(solution)/shard_map/all_gather | solution.py:124
  1611.1 185.6 %reduce-scatter.47.cloned.1.call-start = ((), (), s32[]{:S(2)}) async-start(), calls=%async_computation.32 | async-start | bytes 5898240 | tf_op jit(solution)/shard_map/reduce_scatter | solution.py:134
  1712.5 172.4 %reduce-scatter.63.cloned.1.call-start = ((), (), s32[]{:S(2)}) async-start(), calls=%async_computation.55 | async-start | bytes 4423680 | tf_op jit(solution)/shard_map/reshape.137
  1715.6 219.9 %reduce-scatter.61.cloned.1.call-start = ((), (), s32[]{:S(2)}) async-start(), calls=%async_computation.54 | async-start | bytes 4423680 | tf_op jit(solution)/shard_map/reshape.135
  1802.3 154.7 %reduce-scatter.71.cloned.1.call-start = ((), (), s32[]{:S(2)}) async-start(), calls=%async_computation.59 | async-start | bytes 1327104
  1807.3 183.6 %reduce-scatter.67.cloned.1.call-start = ((), (), s32[]{:S(2)}) async-start(), calls=%async_computation.57 | async-start | bytes 3096576
  1827.8 184.0 %reduce-scatter.69.cloned.1.call-start = ((), (), s32[]{:S(2)}) async-start(), calls=%async_computation.58 | async-start | bytes 1327104
  1832.9 212.6 %reduce-scatter.65.cloned.1.call-start = ((), (), s32[]{:S(2)}) async-start(), calls=%async_computation.56 | async-start | bytes 3096576
  1853.4 233.0 %reduce-scatter.55.cloned.1.call-start = ((), (), s32[]{:S(2)}) async-start(), calls=%async_computation.36 | async-start | bytes 3981312 | tf_op jit(solution)/shard_map/reduce_scatter | solution.py:150
  1860.6 266.1 %reduce-scatter.59.cloned.1.call-start = ((), (), s32[]{:S(2)}) async-start(), calls=%async_computation.38 | async-start | bytes 3981312 | tf_op jit(solution)/shard_map/reduce_scatter | solution.py:153
  1868.7 298.1 %reduce-scatter.57.cloned.1.call-start = ((), (), s32[]{:S(2)}) async-start(), calls=%async_computation.37 | async-start | bytes 3981312 | tf_op jit(solution)/shard_map/reduce_scatter | solution.py:153
  1877.0 330.7 %reduce-scatter.53.cloned.1.call-start = ((), (), s32[]{:S(2)}) async-start(), calls=%async_computation.35 | async-start | bytes 3981312 | tf_op jit(solution)/shard_map/reduce_scatter | solution.py:150
  1884.2 380.1 %reduce-scatter.49.cloned.1.call-start = ((), (), s32[]{:S(2)}) async-start(), calls=%async_computation.33 | async-start | bytes 6193152 | tf_op jit(solution)/shard_map/reduce_scatter | solution.py:141
  1943.1 377.6 %reduce-scatter.51.cloned.1.call-start = ((), (), s32[]{:S(2)}) async-start(), calls=%async_computation.34 | async-start | bytes 6193152 | tf_op jit(solution)/shard_map/reduce_scatter | solution.py:141
  1943.7 531.5 %all-reduce.7.cloned.1.call-start = ((), (), s32[]{:S(2)}) async-start(), calls=%async_computation.60 | async-start | bytes 16515072 | tf_op jit(solution)/shard_map/psum | solution.py:159
  2207.7 345.9 %all-gather.70.cloned.1.call-start = ((), (), s32[]{:S(2)}) async-start(), calls=%async_computation.52 | async-start | bytes 10321920 | tf_op jit(solution)/shard_map/all_gather | solution.py:14
  2264.3 330.3 %all-gather.72.cloned.1.call-start = ((), (), s32[]{:S(2)}) async-start(), calls=%async_computation.53 | async-start | bytes 10321920 | tf_op jit(solution)/shard_map/all_gather | solution.py:14
  (130 other events, 1566.8 us)
Sparse Core Ops, SparseCore 0:
  11.8 58.6 all-gather.43
  72.7 55.9 all-gather.55
  130.8 68.2 all-gather.47
  201.2 49.9 all-gather.45
  285.5 84.0 reduce-scatter.32
  371.5 39.8 all-gather.51
  413.6 49.9 all-gather.49
  465.7 38.1 all-gather.53
  513.6 85.2 reduce-scatter.34
  600.9 68.7 all-gather.57
  671.8 50.0 all-gather.37
  763.3 84.0 reduce-scatter.36
  863.6 50.4 all-gather.39
  915.5 38.1 all-gather.59
  955.1 39.3 all-gather.61
  996.5 49.9 all-gather.63
  1048.7 84.0 reduce-scatter.38
  1135.5 85.7 reduce-scatter.40
  1240.2 50.4 all-gather.65
  1336.7 84.0 reduce-scatter.42
  1453.5 49.5 all-gather.41
  1519.4 84.0 reduce-scatter.44
  1611.2 50.4 all-gather.67
  1712.6 84.0 reduce-scatter.46
  1799.0 67.0 reduce-scatter.62
  1868.8 66.6 reduce-scatter.60
  1938.2 18.7 reduce-scatter.70
  1959.3 31.5 reduce-scatter.66
  1993.1 18.5 reduce-scatter.68
  2013.9 31.5 reduce-scatter.64
  2048.3 38.0 reduce-scatter.54
  2088.6 38.0 reduce-scatter.58
  2128.8 38.0 reduce-scatter.56
  2169.6 38.0 reduce-scatter.52
  2210.6 53.6 reduce-scatter.48
  2267.0 53.6 reduce-scatter.50
  2324.4 150.8 all-reduce.6
  2476.8 58.5 all-gather.69
  2536.8 57.7 all-gather.71
